TPU v7x, 32 devices: a whole 2x2x4 slice. The times are simulated.
32 devices in a mesh: row: 8 (over y, x, core), col: 4 (over z).
Axes of the slice: x: 2, y: 2, z: 4, core: 2. Of those that a mesh axis runs over, the one named last changes fastest.
Arguments:
- chol: float32 [12288, 640], P(('row', 'col')), may hold values from -6 to 6
- eps_occ: float32 [48], replicated, may hold values from -2 to -0.5
- eps_vir: float32 [256], replicated, may hold values from 0.3 to 3
Outputs:
- work: float32 [12288, 640], P(('row', 'col'))
- energies: float32 [2], replicated
All inputs are finite; a program needn't handle non-finite values.
Results may differ from a plain program's by a relative error of at most 0.00013.
Values sent between devices are 32-bit elements; how exact they have to be, the bound alone decides.
A program may use at most 192 MiB of HBM per device.

v0:
```python
import jax
import jax.numpy as jnp
from jax import lax
from jax.sharding import PartitionSpec as P

ITERS = 2


def shards(chol, eps_occ, eps_vir):
    n_row = lax.axis_size("row")
    n_col = lax.axis_size("col")
    row_index = lax.axis_index("row")
    col_index = lax.axis_index("col")
    shard = chol.shape[0]
    width = chol.shape[1]
    occupied = eps_occ.shape[0]
    virtual = eps_vir.shape[0]
    shard_virtuals = shard // occupied
    block_virtuals = n_col * shard_virtuals
    total = virtual * occupied
    row_vir = lax.dynamic_slice_in_dim(eps_vir, row_index * block_virtuals, block_virtuals, 0)
    row_pair = row_vir[:, None] - eps_occ[None, :]
    col_vir = lax.dynamic_slice_in_dim(
        eps_vir.reshape(n_row, block_virtuals), col_index * shard_virtuals, shard_virtuals, 1
    ).reshape(n_row * shard_virtuals)
    col_pair = col_vir[:, None] - eps_occ[None, :]
    chol_cols = lax.all_gather(
        chol.reshape(shard_virtuals, occupied, width), "row", axis=0, tiled=True
    )
    work = jnp.zeros_like(chol)
    sums = []
    for step in range(ITERS):
        factor = chol + work
        rows_factor = lax.all_gather(factor, "col", axis=0, tiled=True)
        piece = lax.all_gather(
            factor.reshape(shard_virtuals, occupied, width), "row", axis=0, tiled=True
        )
        count = piece.shape[0]
        product = lax.dot_general(
            rows_factor,
            piece.reshape(count * occupied, width),
            (((1,), (1,)), ((), ())),
            precision=lax.Precision.HIGHEST,
            preferred_element_type=jnp.float32,
        )
        direct = product.reshape(block_virtuals, occupied, count, occupied)
        numerator = 2.0 * direct - jnp.transpose(direct, (0, 3, 2, 1))
        denominator = row_pair[:, :, None, None] + col_pair[None, None, :, :]
        tile = (-numerator / (jnp.float32(total) * denominator)).reshape(
            block_virtuals * occupied, count * occupied
        )
        chol_piece = chol_cols.reshape(count * occupied, width)
        partial_value = jnp.dot(
            tile, chol_piece, precision=lax.Precision.HIGHEST, preferred_element_type=jnp.float32
        )
        work = lax.psum_scatter(partial_value, "col", scatter_dimension=0, tiled=True)
        local_sum = jnp.sum(chol * work)
        sums.append(local_sum)
    energies = lax.psum(jnp.stack(sums), ("row", "col"))
    return (work, energies / jnp.float32(total))


def solution(mesh):
    placed = (P(("row", "col"), None), P(), P())
    return jax.shard_map(
        shards,
        mesh=mesh,
        in_specs=placed,
        out_specs=(P(("row", "col"), None), P()),
        check_vma=False,
    )
```

profile of v0, /device:TPU:0, one launch (start us, length us, event | category | flops | bytes accessed | tf_op | source)
XLA Modules:
  0.0 1033.4 jit_solution(1675369494210483209)
XLA Ops:
  7.2 0.7 all-gather.5.cloned.1.call-update
  7.9 2.5 copy.8
  10.5 0.8 reshape.90
  11.2 0.8 dynamic_slice.6
  12.0 0.1 constant_dynamic-slice_fusion
  12.1 0.1 sub.46
  12.2 0.7 broadcast_subtract_fusion.1
  12.9 0.7 broadcast_subtract_fusion
  13.6 75.1 %all-gather.5.cloned.1.call-done = f32[1536,640]{1,0:T(8,128)} async-done(((f32[384,640]{1,0:T(8,128)}), f32[1536,640]{1,0:T(8,128)}) %all-gather.5.cloned.1.call-update) | async-done | bytes 3932176 | tf_op jit(solution)/shard_map/all_gather | solution.py:34
  88.7 53.0 %all-gather.7.cloned.1.call-done = f32[64,48,640]{2,0,1:T(8,128)} async-done(((f32[8,48,640]{2,0,1:T(8,128)}), f32[64,48,640]{2,0,1:T(8,128)}) %all-gather.7.cloned.1.call-update) | async-done | bytes 7864336 | tf_op jit(solution)/shard_map/all_gather | solution.py:35
  141.7 94.6 %fusion.6 = f32[32,48,64,48]{2,1,3,0:T(8,128)} fusion(f32[32,48,640,1]{2,1,3,0:T(8,128)} %bitcast.47, f32[64,48,640]{2,0,1:T(8,128)} %all-gather.7.cloned.1.call-done), kind=kOutput, calls=%fused_computation.11 | convolution fusion | flops 36238786560 | bytes 30670848 | tf_op jit(solution)/shard_map/dot_general | solution.py:39
  236.3 38.2 %fusion.3 = f32[32,48,64,48]{2,3,1,0:T(8,128)} fusion(f32[32,48,64,48]{2,1,3,0:T(8,128)} %fusion.6, f32[64,48]{0,1:T(8,128)S(1)} %broadcast_subtract_fusion, f32[32,48]{1,0:T(8,128)S(1)} %broadcast_subtract_fusion.1), kind=kLoop, calls=%fused_computation.5 | loop fusion | flops 28311552 | bytes 37767168 | tf_op jit(solution)/shard_map/div | solution.py:49
  274.5 43.4 %copy.10 = f32[32,48,64,48]{3,2,1,0:T(8,128)} copy(f32[32,48,64,48]{2,3,1,0:T(8,128)} %fusion.3) | data formatting | bytes 37748736 | tf_op jit(solution)/shard_map/div | solution.py:49
  317.9 47.0 %reshape.91 = f32[1536,3072]{1,0:T(8,128)} reshape(f32[32,48,64,48]{3,2,1,0:T(8,128)} %copy.10) | data formatting | bytes 37748736 | tf_op jit(solution)/shard_map/reshape | solution.py:49
  364.9 7.8 copy.11
  372.7 3.0 copy-done.1
  375.7 54.5 %fusion.8 = f32[1536,640]{1,0:T(8,128)} fusion(f32[1536,3072]{1,0:T(8,128)} %reshape.91, f32[3072,640]{1,0:T(8,128)S(1)} %bitcast.45), kind=kOutput, calls=%fused_computation.20 | convolution fusion | flops 36238786560 | bytes 30670848 | tf_op jit(solution)/shard_map/dot_general | solution.py:53
  430.2 72.7 %reduce-scatter.3.cloned.1.call-done = f32[384,640]{1,0:T(8,128)} async-done(((f32[1536,640]{1,0:T(8,128)}), f32[384,640]{1,0:T(8,128)}) %reduce-scatter.3.cloned.1.call-update) | async-done | bytes 983056 | tf_op jit(solution)/shard_map/reduce_scatter | solution.py:56
  503.0 2.2 add.40
  505.3 2.5 copy.12
  507.8 74.4 %all-gather.9.cloned.1.call-done = f32[1536,640]{1,0:T(8,128)} async-done(((f32[384,640]{1,0:T(8,128)}), f32[1536,640]{1,0:T(8,128)}) %all-gather.9.cloned.1.call-update) | async-done | bytes 3932176 | tf_op jit(solution)/shard_map/all_gather | solution.py:34
  582.2 52.2 %all-gather.11.cloned.1.call-done = f32[64,48,640]{2,0,1:T(8,128)} async-done(((f32[8,48,640]{2,0,1:T(8,128)}), f32[64,48,640]{2,0,1:T(8,128)}) %all-gather.11.cloned.1.call-update) | async-done | bytes 7864336 | tf_op jit(solution)/shard_map/all_gather | solution.py:35
  634.5 94.6 %fusion.4 = f32[32,48,64,48]{2,1,3,0:T(8,128)} fusion(f32[32,48,640,1]{2,1,3,0:T(8,128)} %bitcast.48, f32[64,48,640]{2,0,1:T(8,128)} %all-gather.11.cloned.1.call-done), kind=kOutput, calls=%fused_computation.9 | convolution fusion | flops 36238786560 | bytes 30670848 | tf_op jit(solution)/shard_map/dot_general | solution.py:39
  729.1 38.2 %fusion.1 = f32[32,48,64,48]{2,3,1,0:T(8,128)} fusion(f32[32,48,64,48]{2,1,3,0:T(8,128)} %fusion.4, f32[64,48]{0,1:T(8,128)S(1)} %broadcast_subtract_fusion, f32[32,48]{1,0:T(8,128)S(1)} %broadcast_subtract_fusion.1), kind=kLoop, calls=%fused_computation.2 | loop fusion | flops 28311552 | bytes 37767168 | tf_op jit(solution)/shard_map/div | solution.py:49
  767.3 43.4 %copy.14 = f32[32,48,64,48]{3,2,1,0:T(8,128)} copy(f32[32,48,64,48]{2,3,1,0:T(8,128)} %fusion.1) | data formatting | bytes 37748736 | tf_op jit(solution)/shard_map/div | solution.py:49
  810.7 47.0 %reshape.94 = f32[1536,3072]{1,0:T(8,128)} reshape(f32[32,48,64,48]{3,2,1,0:T(8,128)} %copy.14) | data formatting | bytes 37748736 | tf_op jit(solution)/shard_map/reshape | solution.py:49
  857.7 51.2 %fusion.9 = f32[1536,640]{1,0:T(8,128)} fusion(f32[1536,3072]{1,0:T(8,128)} %reshape.94, f32[3072,640]{1,0:T(8,128)} %bitcast.46), kind=kOutput, calls=%fused_computation.21 | convolution fusion | flops 36238786560 | bytes 30670848 | tf_op jit(solution)/shard_map/dot_general | solution.py:53
  908.9 72.8 %reduce-scatter.5.cloned.1.call-done = f32[384,640]{1,0:T(8,128)} async-done(((f32[1536,640]{1,0:T(8,128)}), f32[384,640]{1,0:T(8,128)}) %reduce-scatter.5.cloned.1.call-update) | async-done | bytes 983056 | tf_op jit(solution)/shard_map/reduce_scatter | solution.py:56
  981.7 2.1 multiply_reduce_fusion.1
  983.8 1.3 pad_maximum_fusion
  985.0 40.6 %psum.7 = f32[2]{0:T(128)S(1)} all-reduce(f32[2]{0:T(128)S(1)} %pad_maximum_fusion), channel_id=1, replica_groups=mesh['row'=8,'col'=4] {'row','col'}, use_global_device_ids=true, to_apply=%region_4.0 | all-reduce | flops 2 | bytes 16 | tf_op jit(solution)/shard_map/psum | solution.py:59
  1025.6 0.5 broadcast_multiply_fusion
  (16 shorter events, 0.3 us)
Async XLA Ops:
  7.2 81.6 %all-gather.5.cloned.1.call-start = ((), (), s32[]{:S(2)}) async-start(), calls=%async_computation.2 | async-start | bytes 4915200 | tf_op jit(solution)/shard_map/all_gather | solution.py:34
  7.9 133.8 %all-gather.7.cloned.1.call-start = ((), (), s32[]{:S(2)}) async-start(), calls=%async_computation.3 | async-start | bytes 8847360 | tf_op jit(solution)/shard_map/all_gather | solution.py:35
  10.4 492.5 %reduce-scatter.3.cloned.1.call-start = ((), (), s32[]{:S(2)}) async-start(), calls=%async_computation.4 | async-start | bytes 4915200 | tf_op jit(solution)/shard_map/reduce_scatter | solution.py:56
  372.7 3.0 copy-start.1
  375.7 127.3 %copy-start = (f32[384,640]{1,0:T(8,128)S(1)}, f32[384,640]{1,0:T(8,128)}, u32[]{:S(2)}) copy-start(f32[384,640]{1,0:T(8,128)} %param.3) | copy-start | bytes 2949124
  430.2 152.0 %all-gather.9.cloned.1.call-start = ((), (), s32[]{:S(2)}) async-start(), calls=%async_computation.5 | async-start | bytes 4915200 | tf_op jit(solution)/shard_map/all_gather | solution.py:34
  505.2 129.3 %all-gather.11.cloned.1.call-start = ((), (), s32[]{:S(2)}) async-start(), calls=%async_computation.6 | async-start | bytes 8847360 | tf_op jit(solution)/shard_map/all_gather | solution.py:35
  507.8 473.9 %reduce-scatter.5.cloned.1.call-start = ((), (), s32[]{:S(2)}) async-start(), calls=%async_computation.7 | async-start | bytes 4915200 | tf_op jit(solution)/shard_map/reduce_scatter | solution.py:56
  857.7 124.0 %copy-start.2 = (f32[384,640]{1,0:T(8,128)S(1)}, f32[384,640]{1,0:T(8,128)}, u32[]{:S(2)}) copy-start(f32[384,640]{1,0:T(8,128)} %reduce-scatter.3.cloned.1.call-done) | copy-start | bytes 2949124
Sparse Core Ops, SparseCore 0:
  9.5 79.1 all-gather.4
  91.2 50.4 all-gather.6
  430.3 72.6 reduce-scatter.2
  505.4 76.8 all-gather.8
  584.0 50.4 all-gather.10
  909.0 72.6 reduce-scatter.4
where the time goes:
time: 1050 us; the launch traced here: 1030 us
  waiting for transfers between devices  401 us (38%)
  matrix products  295 us (28%)
  local copies, waits for them, and re-layouts  198 us (19%)
  other arithmetic  84 us (8%)
  blocking collectives  40.6 us (4%)
  between operations  14.5 us (1%)
    dot_general x2, matrix products, shards(): lax.dot_general(rows_factor, piece.reshape(count * occupied, width), (((1...  189 us
    all_gather x2, waiting for transfers between devices, shards(): rows_factor = lax.all_gather(factor, 'col', axis=0, tiled=True)  150 us
    reduce_scatter x2, waiting for transfers between devices, shards(): lax.psum_scatter(partial_value, 'col', scatter_dimension=0, tiled=True)  145 us
    dot_general x2, matrix products, shards(): jnp.dot(tile, chol_piece, precision=lax.Precision.HIGHEST, preferred_elem...  106 us
    all_gather x2, waiting for transfers between devices, shards(): lax.all_gather(factor.reshape(shard_virtuals, occupied, width), 'row', ax...  105 us
    reshape x2, local copies, waits for them, and re-layouts, shards(): (-numerator / (jnp.float32(total) * denominator)).reshape(block_virtuals...  94 us
    div x2, local copies, waits for them, and re-layouts, shards(): -numerator / (jnp.float32(total) * denominator)  86.8 us
    div x2, other arithmetic, shards(): -numerator / (jnp.float32(total) * denominator)  76.5 us
  transfers between devices with their start and end apart: 6, of which 6 were waited for; matrix products, arithmetic and copies ran while one was open for 1% of the time, Pallas kernels for 0%

commit v1 on v0

--- a/solution.py
+++ b/solution.py
@@ -31,7 +31,14 @@
     sums = []
     for step in range(ITERS):
         factor = chol + work
-        rows_factor = lax.all_gather(factor, "col", axis=0, tiled=True)
+        ring = [factor]
+        for hop in range(3):
+            ring.append(lax.ppermute(ring[-1], "col", [(dev, (dev + 1) % 4) for dev in range(4)]))
+        rows_factor = jnp.roll(
+            jnp.concatenate(ring[::-1], axis=0),
+            (lax.axis_index("col") + 1) * ring[0].shape[0],
+            axis=0,
+        )
         piece = lax.all_gather(
             factor.reshape(shard_virtuals, occupied, width), "row", axis=0, tiled=True
         )

time: 1050 us -> 958 us (0.912)
  waiting for transfers between devices: 401 us -> 282 us
  other arithmetic: 84 us -> 103 us
  matrix products: 295 us -> 307 us
    all_gather x2 -> x0, waiting for transfers between devices: 150 us -> none  [shards(): rows_factor = lax.all_gather(factor, 'col', axis=0, tiled=True)]
    ppermute x0 -> x6, waiting for transfers between devices: none -> 140 us  [shards(): lax.ppermute(ring[-1], 'col', [(dev, (dev + 1) % 4) for dev in range(4)])]
    all_gather x2, waiting for transfers between devices: 105 us -> 0.01 us  [shards(): lax.all_gather(factor.reshape(shard_virtuals, occupied, width), 'row', ax...]
    concatenate x0 -> x2, other arithmetic: none -> 19.1 us  [shards(): jnp.roll(jnp.concatenate(ring[::-1], axis=0), (lax.axis_index('col') + 1)...]
    dot_general x2, matrix products: 189 us -> 202 us  [shards(): lax.dot_general(rows_factor, piece.reshape(count * occupied, width), (((1...]
  transfers between devices with their start and end apart: 6 -> 10, of which waited for: 6 -> 8; matrix products, arithmetic and copies ran while one was open for 1% -> 2% of each run, Pallas kernels for 0% -> 0%
where the time goes in v1:
time: 958 us; the launch traced here: 949 us
  matrix products  307 us (32%)
  waiting for transfers between devices  282 us (29%)
  local copies, waits for them, and re-layouts  198 us (21%)
  other arithmetic  103 us (11%)
  blocking collectives  40.6 us (4%)
  between operations  14 us (1%)
    dot_general x2, matrix products, shards(): lax.dot_general(rows_factor, piece.reshape(count * occupied, width), (((1...  202 us
    reduce_scatter x2, waiting for transfers between devices, shards(): lax.psum_scatter(partial_value, 'col', scatter_dimension=0, tiled=True)  141 us
    ppermute x6, waiting for transfers between devices, shards(): lax.ppermute(ring[-1], 'col', [(dev, (dev + 1) % 4) for dev in range(4)])  140 us
    dot_general x2, matrix products, shards(): jnp.dot(tile, chol_piece, precision=lax.Precision.HIGHEST, preferred_elem...  106 us
    reshape x2, local copies, waits for them, and re-layouts, shards(): (-numerator / (jnp.float32(total) * denominator)).reshape(block_virtuals...  94 us
    div x2, local copies, waits for them, and re-layouts, shards(): -numerator / (jnp.float32(total) * denominator)  86.8 us
    div x2, other arithmetic, shards(): -numerator / (jnp.float32(total) * denominator)  77.1 us
    psum x1, blocking collectives, shards(): energies = lax.psum(jnp.stack(sums), ('row', 'col'))  40.6 us
  transfers between devices with their start and end apart: 10, of which 8 were waited for; matrix products, arithmetic and copies ran while one was open for 2% of the time, Pallas kernels for 0%

profile of v1, /device:TPU:0, one launch (start us, length us, event | category | flops | bytes accessed | tf_op | source)
XLA Modules:
  0.0 949.5 jit_solution(5889486162077719520)
XLA Ops:
  7.2 2.5 copy.8
  9.7 3.1 collective-permute-start
  12.9 24.0 %collective-permute-done = f32[384,640]{1,0:T(8,128)S(1)} collective-permute-done((f32[384,640]{1,0:T(8,128)}, f32[384,640]{1,0:T(8,128)S(1)}, u32[]{:S(2)}, u32[]{:S(2)}) %collective-permute-start) | collective-permute-done | bytes 983072 | tf_op jit(solution)/shard_map/ppermute | solution.py:36
  36.8 24.7 %collective-permute-done.1 = f32[384,640]{1,0:T(8,128)S(1)} collective-permute-done((f32[384,640]{1,0:T(8,128)S(1)}, f32[384,640]{1,0:T(8,128)S(1)}, u32[]{:S(2)}, u32[]{:S(2)}) %collective-permute-start.1) | collective-permute-done | bytes 983072 | tf_op jit(solution)/shard_map/ppermute | solution.py:36
  61.6 0.8 reshape.90
  64.7 20.7 %collective-permute-done.2 = f32[384,640]{1,0:T(8,128)S(1)} collective-permute-done((f32[384,640]{1,0:T(8,128)S(1)}, f32[384,640]{1,0:T(8,128)S(1)}, u32[]{:S(2)}, u32[]{:S(2)}) %collective-permute-start.2) | collective-permute-done | bytes 983072 | tf_op jit(solution)/shard_map/ppermute | solution.py:36
  85.4 9.7 %fusion.18 = f32[1536,640]{1,0:T(8,128)} fusion(s32[]{:T(128)S(6)} %select_n.21, f32[384,640]{1,0:T(8,128)S(1)} %collective-permute-done.2, f32[384,640]{1,0:T(8,128)S(1)} %collective-permute-done.1, f32[384,640]{1,0:T(8,128)S(1)} %collective-permute-done, f32[384,640]{1,0:T(8,128)} %param.5), kind=kLoop, calls=%fused_computation.39 | loop fusion | flops 6881280 | bytes 7864324 | tf_op jit(solution)/shard_map/jit(_roll_dynamic)/concatenate | solution.py:37
  95.1 106.9 %fusion.6 = f32[32,48,64,48]{2,1,3,0:T(8,128)} fusion(f32[32,48,640,1]{2,1,3,0:T(8,128)} %bitcast.48, f32[64,48,640]{2,0,1:T(8,128)} %all-gather.3.cloned.1.call-done), kind=kOutput, calls=%fused_computation.27 | convolution fusion | flops 36238786560 | bytes 30670848 | tf_op jit(solution)/shard_map/dot_general | solution.py:46
  202.1 38.6 %fusion.3 = f32[32,48,64,48]{2,3,1,0:T(8,128)} fusion(f32[32,48,64,48]{2,1,3,0:T(8,128)} %fusion.6, f32[64,48]{0,1:T(8,128)S(1)} %broadcast_subtract_fusion, f32[32,48]{1,0:T(8,128)S(1)} %broadcast_subtract_fusion.1), kind=kLoop, calls=%fused_computation.5 | loop fusion | flops 28311552 | bytes 37767168 | tf_op jit(solution)/shard_map/div | solution.py:56
  240.6 43.4 %copy.10 = f32[32,48,64,48]{3,2,1,0:T(8,128)} copy(f32[32,48,64,48]{2,3,1,0:T(8,128)} %fusion.3) | data formatting | bytes 37748736 | tf_op jit(solution)/shard_map/div | solution.py:56
  284.0 47.0 %reshape.91 = f32[1536,3072]{1,0:T(8,128)} reshape(f32[32,48,64,48]{3,2,1,0:T(8,128)} %copy.10) | data formatting | bytes 37748736 | tf_op jit(solution)/shard_map/reshape | solution.py:56
  331.0 7.8 copy.11
  338.8 3.0 copy-done.1
  341.8 54.4 %fusion.22 = f32[1536,640]{1,0:T(8,128)} fusion(f32[1536,3072]{1,0:T(8,128)} %reshape.91, f32[3072,640]{1,0:T(8,128)S(1)} %bitcast.45), kind=kOutput, calls=%fused_computation.50 | convolution fusion | flops 36238786560 | bytes 30670848 | tf_op jit(solution)/shard_map/dot_general | solution.py:60
  396.3 70.5 %reduce-scatter.3.cloned.1.call-done = f32[384,640]{1,0:T(8,128)} async-done(((f32[1536,640]{1,0:T(8,128)}), f32[384,640]{1,0:T(8,128)}) %reduce-scatter.3.cloned.1.call-update) | async-done | bytes 983056 | tf_op jit(solution)/shard_map/reduce_scatter | solution.py:63
  466.9 1.3 add.53
  468.2 1.2 copy.12
  469.5 1.4 collective-permute-start.3
  470.9 23.5 %collective-permute-done.3 = f32[384,640]{1,0:T(8,128)S(1)} collective-permute-done((f32[384,640]{1,0:T(8,128)S(1)}, f32[384,640]{1,0:T(8,128)S(1)}, u32[]{:S(2)}, u32[]{:S(2)}) %collective-permute-start.3) | collective-permute-done | bytes 983072 | tf_op jit(solution)/shard_map/ppermute | solution.py:36
  494.4 24.0 %collective-permute-done.4 = f32[384,640]{1,0:T(8,128)S(1)} collective-permute-done((f32[384,640]{1,0:T(8,128)S(1)}, f32[384,640]{1,0:T(8,128)S(1)}, u32[]{:S(2)}, u32[]{:S(2)}) %collective-permute-start.4) | collective-permute-done | bytes 983072 | tf_op jit(solution)/shard_map/ppermute | solution.py:36
  518.5 0.9 copy-done.3
  519.4 23.3 %collective-permute-done.5 = f32[384,640]{1,0:T(8,128)} collective-permute-done((f32[384,640]{1,0:T(8,128)S(1)}, f32[384,640]{1,0:T(8,128)}, u32[]{:S(2)}, u32[]{:S(2)}) %collective-permute-start.5) | collective-permute-done | bytes 983072 | tf_op jit(solution)/shard_map/ppermute | solution.py:36
  542.7 9.4 fusion.11
  552.1 94.9 %fusion.4 = f32[32,48,64,48]{2,1,3,0:T(8,128)} fusion(f32[32,48,640,1]{2,1,3,0:T(8,128)} %bitcast.47, f32[64,48,640]{2,0,1:T(8,128)} %all-gather.5.cloned.1.call-done), kind=kOutput, calls=%fused_computation.25 | convolution fusion | flops 36238786560 | bytes 30670848 | tf_op jit(solution)/shard_map/dot_general | solution.py:46
  647.1 38.6 %fusion.1 = f32[32,48,64,48]{2,3,1,0:T(8,128)} fusion(f32[32,48,64,48]{2,1,3,0:T(8,128)} %fusion.4, f32[64,48]{0,1:T(8,128)S(1)} %broadcast_subtract_fusion, f32[32,48]{1,0:T(8,128)S(1)} %broadcast_subtract_fusion.1), kind=kLoop, calls=%fused_computation.2 | loop fusion | flops 28311552 | bytes 37767168 | tf_op jit(solution)/shard_map/div | solution.py:56
  685.6 43.4 %copy.14 = f32[32,48,64,48]{3,2,1,0:T(8,128)} copy(f32[32,48,64,48]{2,3,1,0:T(8,128)} %fusion.1) | data formatting | bytes 37748736 | tf_op jit(solution)/shard_map/div | solution.py:56
  729.0 47.0 %reshape.94 = f32[1536,3072]{1,0:T(8,128)} reshape(f32[32,48,64,48]{3,2,1,0:T(8,128)} %copy.14) | data formatting | bytes 37748736 | tf_op jit(solution)/shard_map/reshape | solution.py:56
  776.0 51.2 %fusion.23 = f32[1536,640]{1,0:T(8,128)} fusion(f32[1536,3072]{1,0:T(8,128)} %reshape.94, f32[3072,640]{1,0:T(8,128)} %bitcast.46), kind=kOutput, calls=%fused_computation.51 | convolution fusion | flops 36238786560 | bytes 30670848 | tf_op jit(solution)/shard_map/dot_general | solution.py:60
  827.2 70.9 %reduce-scatter.5.cloned.1.call-done = f32[384,640]{1,0:T(8,128)} async-done(((f32[1536,640]{1,0:T(8,128)}), f32[384,640]{1,0:T(8,128)}) %reduce-scatter.5.cloned.1.call-update) | async-done | bytes 983056 | tf_op jit(solution)/shard_map/reduce_scatter | solution.py:63
  898.1 2.1 multiply_reduce_fusion.1
  900.2 1.4 pad_maximum_fusion
  901.6 40.6 %psum.7 = f32[2]{0:T(128)S(1)} all-reduce(f32[2]{0:T(128)S(1)} %pad_maximum_fusion), channel_id=1, replica_groups=mesh['row'=8,'col'=4] {'row','col'}, use_global_device_ids=true, to_apply=%region_4.6 | all-reduce | flops 2 | bytes 16 | tf_op jit(solution)/shard_map/psum | solution.py:66
  (26 shorter events, 3.1 us)
Async XLA Ops:
  7.2 88.0 %all-gather.3.cloned.1.call-start = ((), (), s32[]{:S(2)}) async-start(), calls=%async_computation.2 | async-start | bytes 8847360 | tf_op jit(solution)/shard_map/all_gather | solution.py:42
  9.7 457.2 %reduce-scatter.3.cloned.1.call-start = ((), (), s32[]{:S(2)}) async-start(), calls=%async_computation.3 | async-start | bytes 4915200 | tf_op jit(solution)/shard_map/reduce_scatter | solution.py:63
  9.7 27.1 %collective-permute-start = (f32[384,640]{1,0:T(8,128)}, f32[384,640]{1,0:T(8,128)S(1)}, u32[]{:S(2)}, u32[]{:S(2)}) collective-permute-start(f32[384,640]{1,0:T(8,128)} %param.5), channel_id=1, source_target_pairs={{0,1},{1,2},{2,3},{3,0},{4,5},{5,6},{6,7},{7,4},{8,9},{9,10},{10,1... | collective-permute-start | bytes 2949128 | tf_op jit(solution)/shard_map/ppermute | solution.py:36
  36.8 24.7 %collective-permute-start.1 = (f32[384,640]{1,0:T(8,128)S(1)}, f32[384,640]{1,0:T(8,128)S(1)}, u32[]{:S(2)}, u32[]{:S(2)}) collective-permute-start(f32[384,640]{1,0:T(8,128)S(1)} %collective-permute-done), channel_id=1, source_target_pairs={{0,1},{1,2},{2,3},{3,0},{4,5},{5,6},{6,7},{7,4},{8,9},{9,10},{10,1... | collective-permute-start | bytes 2949128 | tf_op jit(solution)/shard_map/ppermute | solution.py:36
  61.6 23.9 %collective-permute-start.2 = (f32[384,640]{1,0:T(8,128)S(1)}, f32[384,640]{1,0:T(8,128)S(1)}, u32[]{:S(2)}, u32[]{:S(2)}) collective-permute-start(f32[384,640]{1,0:T(8,128)S(1)} %collective-permute-done.1), channel_id=1, source_target_pairs={{0,1},{1,2},{2,3},{3,0},{4,5},{5,6},{6,7},{7,4},{8,9},{9,10},{10,1... | collective-permute-start | bytes 2949128 | tf_op jit(solution)/shard_map/ppermute | solution.py:36
  338.8 3.0 copy-start.1
  341.8 125.0 %copy-start = (f32[384,640]{1,0:T(8,128)S(1)}, f32[384,640]{1,0:T(8,128)}, u32[]{:S(2)}) copy-start(f32[384,640]{1,0:T(8,128)} %param.5) | copy-start | bytes 2949124
  396.3 155.8 %all-gather.5.cloned.1.call-start = ((), (), s32[]{:S(2)}) async-start(), calls=%async_computation.4 | async-start | bytes 8847360 | tf_op jit(solution)/shard_map/all_gather | solution.py:42
  469.4 428.7 %reduce-scatter.5.cloned.1.call-start = ((), (), s32[]{:S(2)}) async-start(), calls=%async_computation.5 | async-start | bytes 4915200 | tf_op jit(solution)/shard_map/reduce_scatter | solution.py:63
  469.5 25.0 %collective-permute-start.3 = (f32[384,640]{1,0:T(8,128)S(1)}, f32[384,640]{1,0:T(8,128)S(1)}, u32[]{:S(2)}, u32[]{:S(2)}) collective-permute-start(f32[384,640]{1,0:T(8,128)S(1)} %add.53), channel_id=1, source_target_pairs={{0,1},{1,2},{2,3},{3,0},{4,5},{5,6},{6,7},{7,4},{8,9},{9,10},{10,1... | collective-permute-start | bytes 2949128 | tf_op jit(solution)/shard_map/ppermute | solution.py:36
  494.4 24.0 %collective-permute-start.4 = (f32[384,640]{1,0:T(8,128)S(1)}, f32[384,640]{1,0:T(8,128)S(1)}, u32[]{:S(2)}, u32[]{:S(2)}) collective-permute-start(f32[384,640]{1,0:T(8,128)S(1)} %collective-permute-done.3), channel_id=1, source_target_pairs={{0,1},{1,2},{2,3},{3,0},{4,5},{5,6},{6,7},{7,4},{8,9},{9,10},{10,1... | collective-permute-start | bytes 2949128 | tf_op jit(solution)/shard_map/ppermute | solution.py:36
  518.5 0.9 copy-start.3
  519.4 23.3 %collective-permute-start.5 = (f32[384,640]{1,0:T(8,128)S(1)}, f32[384,640]{1,0:T(8,128)}, u32[]{:S(2)}, u32[]{:S(2)}) collective-permute-start(f32[384,640]{1,0:T(8,128)S(1)} %collective-permute-done.4), channel_id=1, source_target_pairs={{0,1},{1,2},{2,3},{3,0},{4,5},{5,6},{6,7},{7,4},{8,9},{9,10},{10,1... | collective-permute-start | bytes 2949128 | tf_op jit(solution)/shard_map/ppermute | solution.py:36
  776.0 122.1 %copy-start.2 = (f32[384,640]{1,0:T(8,128)S(1)}, f32[384,640]{1,0:T(8,128)}, u32[]{:S(2)}) copy-start(f32[384,640]{1,0:T(8,128)} %reduce-scatter.3.cloned.1.call-done) | copy-start | bytes 2949124
Sparse Core Ops, SparseCore 0:
  10.4 54.6 all-gather.2
  396.4 70.3 reduce-scatter.2
  469.6 52.3 all-gather.4
  827.3 70.7 reduce-scatter.4
